TPU v7x, 256 devices: a whole 4x4x8 slice. The times are simulated.
256 devices in a mesh: box: 32 (over x, z), pencil: 8 (over y, core).
Axes of the slice: x: 4, y: 4, z: 8, core: 2. Of those that a mesh axis runs over, the one named last changes fastest.
Arguments:
- previous: bfloat16 [32, 256, 256, 128], P('box', 'pencil'), may hold values from -48 to 48
- source: bfloat16 [32, 256, 256, 128], P('box', 'pencil'), may hold values from -48 to 48
- neighbor: int32 [32, 2, 16], replicated, may hold values from 0 to 31, as said below
- depth: int32 [32, 2, 16], replicated, may hold values from 1 to 8
- wall: int32 [32, 2, 256], P('box', None, 'pencil'), may hold values 0 or 1
Outputs:
- solution: float32 [32, 256, 256, 128], P('box', 'pencil')
Inputs may be any that keep to these rules, and one draw needn't show every extreme that they name: For each face and segment, neighbor[:, face, segment] is a permutation of the 32 boxes in which no box names itself.
All inputs are finite; a program needn't handle non-finite values. No bound on the sum of `wall` on one device may be relied on, other than what follows from the above.
Results may differ from a plain program's by a relative error of at most 0.014.
Values may be sent and summed in bfloat16 or wider, within the bound.
A program may use at most 64 MiB of HBM per device.

v0:
```python
import jax
import jax.numpy as jnp
from jax import lax
from jax.sharding import PartitionSpec as P

W = 8
ITERS = 2
REFLECT = 0.6
TIMESTEP = 64.0


def sine_table(length):
    ordinal = jnp.arange(length, dtype=jnp.float32) + 1.0
    phase_angle = jnp.pi * ordinal[:, None] * ordinal[None, :] / (length + 1.0)
    return (jnp.sqrt(2.0 / (length + 1.0)) * jnp.sin(phase_angle)).astype(jnp.bfloat16)


def eigen_values(length):
    ordinal = jnp.arange(length, dtype=jnp.float32) + 1.0
    return 2.0 - 2.0 * jnp.cos(jnp.pi * ordinal / (length + 1.0))


def shards(previous, source, neighbor, depth, wall):
    pencils = lax.axis_size("pencil")
    pencil_index = lax.axis_index("pencil")
    box_index = lax.axis_index("box")
    plane_count = previous.shape[1]
    column_count = previous.shape[2]
    depth_count = previous.shape[3]
    length_all = plane_count * pencils
    segment_count = neighbor.shape[2]
    segment_length = length_all // segment_count
    length_table = sine_table(length_all)
    width_table = sine_table(column_count)
    depth_table = sine_table(depth_count)
    length_eigen = eigen_values(length_all)
    width_eigen = eigen_values(column_count)
    depth_eigen = eigen_values(depth_count)
    forcing = previous[0].astype(jnp.float32) + source[0].astype(jnp.float32)
    positions = jnp.arange(plane_count, dtype=jnp.int32)
    global_planes = pencil_index * plane_count + positions
    segment_hit = (global_planes // segment_length)[:, None] == jnp.arange(
        segment_count, dtype=jnp.int32
    )[None, :]
    own_lists = lax.dynamic_index_in_dim(neighbor, box_index, 0, keepdims=False)
    own_depths = lax.dynamic_index_in_dim(depth, box_index, 0, keepdims=False)
    donor_box = jnp.sum(jnp.where(segment_hit[None], own_lists[:, None, :], 0), axis=2)
    donor_depth = jnp.sum(jnp.where(segment_hit[None], own_depths[:, None, :], 0), axis=2)
    end_planes = ((global_planes == 0) | (global_planes == length_all - 1)).astype(jnp.float32)[
        :, None, None
    ]
    wall_local = wall[0]
    current = previous[0]
    solved = None
    for iteration in range(ITERS):
        iterate = current.astype(jnp.float32)
        high_band = current[:, column_count - 1 - W : column_count - 1, :][:, ::-1, :]
        low_band = current[:, 1 : W + 1, :]
        export = jnp.concatenate([high_band, low_band], axis=1)
        gathered = lax.all_gather(export, "box", axis=0, tiled=True)
        low_import = gathered[donor_box[0] * plane_count + positions, donor_depth[0] - 1, :]
        high_import = gathered[donor_box[1] * plane_count + positions, W + donor_depth[1] - 1, :]
        low_ghost = jnp.where(
            wall_local[0][:, None] == 1, REFLECT * iterate[:, 0, :], low_import.astype(jnp.float32)
        )
        high_ghost = jnp.where(
            wall_local[1][:, None] == 1,
            REFLECT * iterate[:, column_count - 1, :],
            high_import.astype(jnp.float32),
        )
        boundary = jnp.zeros_like(iterate)
        boundary = boundary.at[:, 0, :].add(low_ghost)
        boundary = boundary.at[:, column_count - 1, :].add(high_ghost)
        boundary = boundary + end_planes * (REFLECT * iterate)
        boundary = boundary.at[:, :, 0].add(REFLECT * iterate[:, :, 0])
        boundary = boundary.at[:, :, depth_count - 1].add(REFLECT * iterate[:, :, depth_count - 1])
        right_side = (forcing + TIMESTEP * boundary).astype(jnp.bfloat16)
        first_pass = jnp.einsum(
            "xyz,zk->xyk", right_side, depth_table, preferred_element_type=jnp.float32
        ).astype(jnp.bfloat16)
        second_pass = jnp.einsum(
            "xyz,yk->xkz", first_pass, width_table, preferred_element_type=jnp.float32
        ).astype(jnp.bfloat16)
        spread = lax.all_to_all(second_pass, "pencil", split_axis=1, concat_axis=0, tiled=True)
        width_part = spread.shape[1]
        width_slice = lax.dynamic_slice_in_dim(width_eigen, pencil_index * width_part, width_part)
        spectrum = 1.0 + TIMESTEP * (
            length_eigen[:, None, None] + width_slice[None, :, None] + depth_eigen[None, None, :]
        )
        third_pass = jnp.einsum(
            "xyz,xk->kyz", spread, length_table, preferred_element_type=jnp.float32
        )
        fourth_pass = (third_pass / spectrum).astype(jnp.bfloat16)
        fifth_pass = jnp.einsum(
            "xyz,xk->kyz", fourth_pass, length_table, preferred_element_type=jnp.float32
        ).astype(jnp.bfloat16)
        returned = lax.all_to_all(fifth_pass, "pencil", split_axis=0, concat_axis=1, tiled=True)
        sixth_pass = jnp.einsum(
            "xyz,yk->xkz", returned, width_table, preferred_element_type=jnp.float32
        ).astype(jnp.bfloat16)
        solved = jnp.einsum(
            "xyz,zk->xyk", sixth_pass, depth_table, preferred_element_type=jnp.float32
        )
        current = solved.astype(jnp.bfloat16)
    return solved[None]


def solution(mesh):
    placed = (
        P("box", "pencil", None, None),
        P("box", "pencil", None, None),
        P(),
        P(),
        P("box", None, "pencil"),
    )
    return jax.shard_map(
        shards,
        mesh=mesh,
        in_specs=placed,
        out_specs=P("box", "pencil", None, None),
        check_vma=False,
    )
```

profile of v0, /device:TPU:1, one launch (start us, length us, event | category | flops | bytes accessed | tf_op | source)
XLA Modules:
  0.0 454.8 jit_solution(6380604464187133774)
XLA Ops:
  10.2 4.2 bitcast_convert_fusion
  14.5 77.5 %all-gather.3.cloned.1.call-done = bf16[1024,16,128]{2,1,0:T(8,128)(2,1)} async-done(((bf16[32,16,128]{2,1,0:T(8,128)(2,1)}), bf16[1024,16,128]{2,1,0:T(8,128)(2,1)}) %all-gather.3.cloned.1.call-update) | async-done | bytes 4194320 | tf_op jit(solution)/shard_map/all_gather | solution.py:60
  95.9 2.4 scatter-add.26
  99.9 3.0 multiply_add_fusion.2
  104.9 2.6 fusion.3
  107.5 10.9 %scatter-add.30 = f32[32,256,128]{2,1,0:T(8,128)} dynamic-update-slice(f32[32,256,128]{2,1,0:T(8,128)} %copy-done.1, f32[32,256,1]{2,1,0:T(8,128)} %fusion.3, s32[]{:T(128)} %constant.259.clone.1, s32[]{:T(128)} %constant.259.clone.1, s32[]{:T(128)} %constant.259.clone.1) | dynamic-update-slice | bytes 65540 | tf_op jit(solution)/shard_map/scatter-add | solution.py:75
  118.4 7.7 %fusion.2 = f32[32,256,1]{2,1,0:T(8,128)} fusion(f32[32,256,128]{2,1,0:T(8,128)} %bitcast_convert_fusion, f32[32,256,128]{2,1,0:T(8,128)} %scatter-add.30), kind=kLoop, calls=%fused_computation.9 | loop fusion | flops 16384 | bytes 98304 | tf_op jit(solution)/shard_map/add | solution.py:76
  126.1 13.0 %scatter-add.31 = f32[32,256,128]{2,1,0:T(8,128)} dynamic-update-slice(f32[32,256,128]{2,1,0:T(8,128)} %scatter-add.30, f32[32,256,1]{2,1,0:T(8,128)} %fusion.2, s32[]{:T(128)} %constant.259.clone.1, s32[]{:T(128)} %constant.259.clone.1, s32[]{:T(128)} %constant.270.clone.1) | dynamic-update-slice | bytes 65540 | tf_op jit(solution)/shard_map/scatter-add | solution.py:76
  139.1 6.7 %convert_bitcast_fusion.1 = bf16[32,256,128]{2,1,0:T(8,128)(2,1)} fusion(f32[32,256,128]{2,1,0:T(8,128)} %scatter-add.31, bf16[1,32,256,128]{3,2,1,0:T(8,128)(2,1)} %param.22, f32[256]{0:T(256)S(1)} %get-tuple-element.119, f32[256]{0:T(256)S(1)} %get-tuple-element.120, f32[128]{0:T(128)S(1)} %get-tuple-element.121, f32[128]{0:T(128)S(1)} %get-tuple-element.122, ...), kind=kOutput, calls=%fused_computation.38 | convolution fusion | flops 814022656 | bytes 10488832 | tf_op jit(solution)/shard_map/xyz,yk->xkz/dot_general | solution.py:81
  145.8 4.3 copy.28
  150.1 8.5 %all-to-all-start = ((bf16[32,256,128]{2,0,1:T(8,128)(2,1)}), bf16[32,256,128]{2,0,1:T(8,128)(2,1)}, u32[]{:S(2)}, u32[]{:S(2)}) async-start(bf16[32,256,128]{2,0,1:T(8,128)(2,1)} %copy.28), calls=%async_computation | async-start | bytes 4194304 | tf_op jit(solution)/shard_map/all_to_all | solution.py:84
  159.3 25.6 %all-to-all-done = bf16[32,256,128]{2,0,1:T(8,128)(2,1)} async-done(((bf16[32,256,128]{2,0,1:T(8,128)(2,1)}), bf16[32,256,128]{2,0,1:T(8,128)(2,1)}, u32[]{:S(2)}, u32[]{:S(2)}) %all-to-all-start) | async-done | bytes 2097184 | tf_op jit(solution)/shard_map/all_to_all | solution.py:84
  184.9 3.7 copy.30
  188.6 6.9 %fusion.32 = bf16[256,32,128]{2,0,1:T(8,128)(2,1)} fusion(f32[128]{0:T(128)S(1)} %multiply_subtract_fusion.1, f32[256,32]{0,1:T(8,128)S(1)} %broadcast_add_fusion, bf16[256,32,128]{2,1,0:T(8,128)(2,1)} %bitcast.148, f32[256]{0:T(256)S(1)} %get-tuple-element.119, f32[256]{0:T(256)S(1)} %get-tuple-element.120), kind=kOutput, calls=%fused_computation.47 | convolution fusion | flops 1080557568 | bytes 4229632 | tf_op jit(solution)/shard_map/xyz,xk->kyz/dot_general | solution.py:94
  195.4 2.9 copy.32
  198.4 29.8 %all_to_all.72 = bf16[256,32,128]{2,1,0:T(8,128)(2,1)S(1)} all-to-all(bf16[256,32,128]{2,1,0:T(8,128)(2,1)S(1)} %copy.32), channel_id=1, replica_groups=mesh['box'=32,'pencil'=8] {'pencil'}, dimensions={0} | all-to-all | bytes 4194304 | tf_op jit(solution)/shard_map/all_to_all | solution.py:97
  228.2 2.0 copy.33
  230.1 6.5 %fusion.171 = (f32[32,256,128]{2,1,0:T(8,128)}, bf16[32,256,128]{2,1,0:T(8,128)(2,1)}) fusion(f32[128]{0:T(128)S(1)} %get-tuple-element.121, f32[128]{0:T(128)S(1)} %get-tuple-element.122, bf16[32,256,128]{2,1,0:T(8,128)(2,1)} %bitcast.142, f32[256]{0:T(256)S(1)} %get-tuple-element.119, f32[256]{0:T(256)S(1)} %get-tuple-element.120), kind=kOutput, calls=%fused_computation.160 | convolution fusion | flops 808779776 | bytes 8391680 | tf_op jit(solution)/shard_map/xyz,zk->xyk/dot_general | solution.py:101
  238.4 73.6 %all-gather.5.cloned.1.call-done = bf16[1024,16,128]{2,1,0:T(8,128)(2,1)} async-done(((bf16[32,16,128]{2,1,0:T(8,128)(2,1)}), bf16[1024,16,128]{2,1,0:T(8,128)(2,1)}) %all-gather.5.cloned.1.call-update) | async-done | bytes 4194320 | tf_op jit(solution)/shard_map/all_gather | solution.py:60
  316.0 2.4 scatter-add.34
  320.0 3.7 multiply_add_fusion
  325.7 2.6 fusion.1
  328.3 10.9 %scatter-add.36 = f32[32,256,128]{2,1,0:T(8,128)} dynamic-update-slice(f32[32,256,128]{2,1,0:T(8,128)} %copy-done, f32[32,256,1]{2,1,0:T(8,128)} %fusion.1, s32[]{:T(128)} %constant.259.clone.1, s32[]{:T(128)} %constant.259.clone.1, s32[]{:T(128)} %constant.259.clone.1) | dynamic-update-slice | bytes 65540 | tf_op jit(solution)/shard_map/scatter-add | solution.py:75
  339.2 7.7 %fusion = f32[32,256,1]{2,1,0:T(8,128)} fusion(f32[32,256,128]{2,1,0:T(8,128)} %get-tuple-element.115, f32[32,256,128]{2,1,0:T(8,128)} %scatter-add.36), kind=kLoop, calls=%fused_computation.5 | loop fusion | flops 16384 | bytes 98304 | tf_op jit(solution)/shard_map/add | solution.py:76
  346.9 13.0 %scatter-add.39 = f32[32,256,128]{2,1,0:T(8,128)} dynamic-update-slice(f32[32,256,128]{2,1,0:T(8,128)} %scatter-add.36, f32[32,256,1]{2,1,0:T(8,128)} %fusion, s32[]{:T(128)} %constant.259.clone.1, s32[]{:T(128)} %constant.259.clone.1, s32[]{:T(128)} %constant.270.clone.1) | dynamic-update-slice | bytes 65540 | tf_op jit(solution)/shard_map/scatter-add | solution.py:76
  359.9 6.7 %convert_bitcast_fusion = bf16[32,256,128]{2,1,0:T(8,128)(2,1)} fusion(f32[32,256,128]{2,1,0:T(8,128)} %scatter-add.39, bf16[1,32,256,128]{3,2,1,0:T(8,128)(2,1)} %param.22, f32[256]{0:T(256)S(1)} %get-tuple-element.119, f32[256]{0:T(256)S(1)} %get-tuple-element.120, f32[128]{0:T(128)S(1)} %get-tuple-element.121, f32[128]{0:T(128)S(1)} %get-tuple-element.122, ...), kind=kOutput, calls=%fused_computation.33 | convolution fusion | flops 814022656 | bytes 10488832 | tf_op jit(solution)/shard_map/xyz,yk->xkz/dot_general | solution.py:81
  366.6 2.9 copy.34
  369.5 34.7 %all_to_all.73 = bf16[32,256,128]{2,0,1:T(8,128)(2,1)S(1)} all-to-all(bf16[32,256,128]{2,0,1:T(8,128)(2,1)S(1)} %copy.34), channel_id=1, replica_groups=mesh['box'=32,'pencil'=8] {'pencil'}, dimensions={1} | all-to-all | bytes 4194304 | tf_op jit(solution)/shard_map/all_to_all | solution.py:84
  405.0 5.2 %fusion.31 = bf16[256,32,128]{2,0,1:T(8,128)(2,1)} fusion(f32[128]{0:T(128)S(1)} %multiply_subtract_fusion.1, f32[256,32]{0,1:T(8,128)S(1)} %broadcast_add_fusion, bf16[256,32,128]{2,1,0:T(8,128)(2,1)S(1)} %bitcast.147, f32[256]{0:T(256)S(1)} %get-tuple-element.119, f32[256]{0:T(256)S(1)} %get-tuple-element.120), kind=kOutput, calls=%fused_computation.46 | convolution fusion | flops 1080557568 | bytes 4229632 | tf_op jit(solution)/shard_map/xyz,xk->kyz/dot_general | solution.py:94
  410.2 2.9 copy.38
  413.2 29.7 %all_to_all.74 = bf16[256,32,128]{2,1,0:T(8,128)(2,1)S(1)} all-to-all(bf16[256,32,128]{2,1,0:T(8,128)(2,1)S(1)} %copy.38), channel_id=1, replica_groups=mesh['box'=32,'pencil'=8] {'pencil'}, dimensions={0} | all-to-all | bytes 4194304 | tf_op jit(solution)/shard_map/all_to_all | solution.py:97
  443.5 4.2 convolution_bitcast_fusion
  (47 shorter events, 22.5 us)
Async XLA Ops:
  6.5 85.4 %all-gather.3.cloned.1.call-start = ((), (), s32[]{:S(2)}) async-start(), calls=%async_computation.4 | async-start | bytes 4325376 | tf_op jit(solution)/shard_map/all_gather | solution.py:60
  10.2 89.7 %copy-start.4 = (bf16[1,32,256,128]{3,2,1,0:T(8,128)(2,1)S(1)}, bf16[1,32,256,128]{3,2,1,0:T(8,128)(2,1)}, u32[]{:S(2)}) copy-start(bf16[1,32,256,128]{3,2,1,0:T(8,128)(2,1)} %param.21) | copy-start | bytes 6291460
  99.9 5.0 %copy-start.3 = (f32[32,256,128]{2,1,0:T(8,128)S(1)}, f32[32,256,128]{2,1,0:T(8,128)}, u32[]{:S(2)}) copy-start(f32[32,256,128]{2,1,0:T(8,128)} %bitcast_convert_fusion) | copy-start | bytes 12582916
  103.0 2.0 copy-start.1
  150.1 34.8 %all-to-all-start = ((bf16[32,256,128]{2,0,1:T(8,128)(2,1)}), bf16[32,256,128]{2,0,1:T(8,128)(2,1)}, u32[]{:S(2)}, u32[]{:S(2)}) async-start(bf16[32,256,128]{2,0,1:T(8,128)(2,1)} %copy.28), calls=%async_computation | async-start | bytes 4194304 | tf_op jit(solution)/shard_map/all_to_all | solution.py:84
  158.6 153.5 %all-gather.5.cloned.1.call-start = ((), (), s32[]{:S(2)}) async-start(), calls=%async_computation.5 | async-start | bytes 4325376 | tf_op jit(solution)/shard_map/all_gather | solution.py:60
  320.0 5.7 %copy-start.2 = (f32[32,256,128]{2,1,0:T(8,128)S(1)}, f32[32,256,128]{2,1,0:T(8,128)}, u32[]{:S(2)}) copy-start(f32[32,256,128]{2,1,0:T(8,128)} %get-tuple-element.115) | copy-start | bytes 12582916
  323.7 2.0 copy-start
Sparse Core Ops, SparseCore 0:
  9.9 81.9 all-gather.2
  238.5 73.4 all-gather.4
where the time goes:
time: 464 us; the launch traced here: 455 us
  waiting for transfers between devices  177 us (38%)
  blocking collectives  94.1 us (20%)
  local copies, waits for them, and re-layouts  88.9 us (19%)
  matrix products  36.3 us (8%)
  other arithmetic  36.1 us (8%)
  between operations  13.8 us (3%)
  starting transfers between devices  8.93 us (2%)
    all_gather x2, waiting for transfers between devices, shards(): gathered = lax.all_gather(export, 'box', axis=0, tiled=True)  151 us
    all_to_all x2, blocking collectives, shards(): lax.all_to_all(fifth_pass, 'pencil', split_axis=0, concat_axis=1, tiled=T...  59.4 us
    all_to_all x1, blocking collectives, shards(): lax.all_to_all(second_pass, 'pencil', split_axis=1, concat_axis=0, tiled=...  34.7 us
    scatter-add x2, local copies, waits for them, and re-layouts, shards(): boundary.at[:, :, depth_count - 1]  26 us
    all_to_all x1, waiting for transfers between devices, shards(): lax.all_to_all(second_pass, 'pencil', split_axis=1, concat_axis=0, tiled=...  25.6 us
    scatter-add x2, local copies, waits for them, and re-layouts, shards(): boundary = boundary.at[:, :, 0].add(REFLECT * iterate[:, :, 0])  21.9 us
    add x2, other arithmetic, shards(): boundary.at[:, :, depth_count - 1]  15.3 us
    dot_general x2, matrix products, shards(): jnp.einsum('xyz,yk->xkz', first_pass, width_table, preferred_element_type...  13.4 us
  transfers between devices with their start and end apart: 3, of which 3 were waited for; matrix products, arithmetic and copies ran while one was open for 1% of the time, Pallas kernels for 0%

commit v1 on v0

--- a/solution.py
+++ b/solution.py
@@ -57,7 +57,16 @@
         high_band = current[:, column_count - 1 - W : column_count - 1, :][:, ::-1, :]
         low_band = current[:, 1 : W + 1, :]
         export = jnp.concatenate([high_band, low_band], axis=1)
-        gathered = lax.all_gather(export, "box", axis=0, tiled=True)
+        levels_all_scan = lambda t0, named_axis: jnp.concatenate(
+            lax.all_to_all(
+                jnp.stack([t0 for _ in range(lax.axis_size(named_axis))]),
+                axis_name=named_axis,
+                split_axis=0,
+                concat_axis=0,
+            ),
+            axis=0,
+        )
+        gathered = levels_all_scan(export, named_axis="box")
         low_import = gathered[donor_box[0] * plane_count + positions, donor_depth[0] - 1, :]
         high_import = gathered[donor_box[1] * plane_count + positions, W + donor_depth[1] - 1, :]
         low_ghost = jnp.where(

time: 464 us -> 499 us (1.075)
  blocking collectives: 94.1 us -> 190 us
  waiting for transfers between devices: 177 us -> 116 us
  starting transfers between devices: 8.93 us -> 22.5 us
  between operations: 13.8 us -> 0.44 us
    all_gather x2 -> x0, waiting for transfers between devices: 151 us -> none  [shards(): gathered = lax.all_gather(export, 'box', axis=0, tiled=True)]
    all_to_all x0 -> x1, blocking collectives: none -> 97.3 us  [shards(): lax.all_to_all(jnp.stack([t0 for _ in range(lax.axis_size(named_axis))]),...]
    all_to_all x0 -> x1, waiting for transfers between devices: none -> 89.6 us  [shards(): lax.all_to_all(jnp.stack([t0 for _ in range(lax.axis_size(named_axis))]),...]
    all_to_all x0 -> x1, starting transfers between devices: none -> 12.1 us  [shards(): lax.all_to_all(jnp.stack([t0 for _ in range(lax.axis_size(named_axis))]),...]
  transfers between devices with their start and end apart: 3 -> 2, of which waited for: 3 -> 2; matrix products, arithmetic and copies ran while one was open for 1% -> 1% of each run, Pallas kernels for 0% -> 0%
where the time goes in v1:
time: 499 us; the launch traced here: 489 us
  blocking collectives  190 us (38%)
  waiting for transfers between devices  116 us (23%)
  local copies, waits for them, and re-layouts  92.2 us (18%)
  matrix products  36.3 us (7%)
  other arithmetic  32.2 us (6%)
  starting transfers between devices  22.5 us (5%)
    all_to_all x1, blocking collectives, shards(): lax.all_to_all(jnp.stack([t0 for _ in range(lax.axis_size(named_axis))]),...  97.3 us
    all_to_all x1, waiting for transfers between devices, shards(): lax.all_to_all(jnp.stack([t0 for _ in range(lax.axis_size(named_axis))]),...  89.6 us
    all_to_all x2, blocking collectives, shards(): lax.all_to_all(fifth_pass, 'pencil', split_axis=0, concat_axis=1, tiled=T...  59.2 us
    all_to_all x1, blocking collectives, shards(): lax.all_to_all(second_pass, 'pencil', split_axis=1, concat_axis=0, tiled=...  33.4 us
    scatter-add x2, local copies, waits for them, and re-layouts, shards(): boundary.at[:, :, depth_count - 1]  26 us
    all_to_all x1, waiting for transfers between devices, shards(): lax.all_to_all(second_pass, 'pencil', split_axis=1, concat_axis=0, tiled=...  26 us
    scatter-add x2, local copies, waits for them, and re-layouts, shards(): boundary = boundary.at[:, :, 0].add(REFLECT * iterate[:, :, 0])  21.9 us
    add x2, other arithmetic, shards(): boundary.at[:, :, depth_count - 1]  15.3 us
  transfers between devices with their start and end apart: 2, of which 2 were waited for; matrix products, arithmetic and copies ran while one was open for 1% of the time, Pallas kernels for 0%

profile of v1, /device:TPU:1, one launch (start us, length us, event | category | flops | bytes accessed | tf_op | source)
XLA Modules:
  0.0 489.3 jit_solution(10438752862346802182)
XLA Ops:
  1.1 3.0 stack.4
  4.1 12.1 %all-to-all-start = ((bf16[32,32,16,128]{3,2,1,0:T(8,128)(2,1)}), bf16[32,32,16,128]{3,2,1,0:T(8,128)(2,1)}, u32[]{:S(2)}, u32[]{:S(2)}) async-start(bf16[32,32,16,128]{3,2,1,0:T(8,128)(2,1)} %stack.4), calls=%async_computation | async-start | bytes 8388608 | tf_op jit(solution)/shard_map/all_to_all | solution.py:61
  19.1 89.6 %all-to-all-done = bf16[32,32,16,128]{3,2,1,0:T(8,128)(2,1)} async-done(((bf16[32,32,16,128]{3,2,1,0:T(8,128)(2,1)}), bf16[32,32,16,128]{3,2,1,0:T(8,128)(2,1)}, u32[]{:S(2)}, u32[]{:S(2)}) %all-to-all-start) | async-done | bytes 4194336 | tf_op jit(solution)/shard_map/all_to_all | solution.py:61
  112.6 2.5 scatter-add.26
  116.7 3.0 multiply_add_fusion.2
  121.8 2.6 fusion.3
  124.4 10.9 %scatter-add.30 = f32[32,256,128]{2,1,0:T(8,128)} dynamic-update-slice(f32[32,256,128]{2,1,0:T(8,128)} %copy-done.1, f32[32,256,1]{2,1,0:T(8,128)} %fusion.3, s32[]{:T(128)} %constant.259.clone.1, s32[]{:T(128)} %constant.259.clone.1, s32[]{:T(128)} %constant.259.clone.1) | dynamic-update-slice | bytes 65540 | tf_op jit(solution)/shard_map/scatter-add | solution.py:84
  135.3 7.7 %fusion.2 = f32[32,256,1]{2,1,0:T(8,128)} fusion(f32[32,256,128]{2,1,0:T(8,128)} %bitcast_convert_fusion, f32[32,256,128]{2,1,0:T(8,128)} %scatter-add.30), kind=kLoop, calls=%fused_computation.9 | loop fusion | flops 16384 | bytes 98304 | tf_op jit(solution)/shard_map/add | solution.py:85
  143.0 13.0 %scatter-add.31 = f32[32,256,128]{2,1,0:T(8,128)} dynamic-update-slice(f32[32,256,128]{2,1,0:T(8,128)} %scatter-add.30, f32[32,256,1]{2,1,0:T(8,128)} %fusion.2, s32[]{:T(128)} %constant.259.clone.1, s32[]{:T(128)} %constant.259.clone.1, s32[]{:T(128)} %constant.270.clone.1) | dynamic-update-slice | bytes 65540 | tf_op jit(solution)/shard_map/scatter-add | solution.py:85
  156.0 6.7 %convert_bitcast_fusion.1 = bf16[32,256,128]{2,1,0:T(8,128)(2,1)} fusion(f32[32,256,128]{2,1,0:T(8,128)} %scatter-add.31, bf16[1,32,256,128]{3,2,1,0:T(8,128)(2,1)} %param.22, f32[256]{0:T(256)S(1)} %get-tuple-element.119, f32[256]{0:T(256)S(1)} %get-tuple-element.120, f32[128]{0:T(128)S(1)} %get-tuple-element.121, f32[128]{0:T(128)S(1)} %get-tuple-element.122, ...), kind=kOutput, calls=%fused_computation.38 | convolution fusion | flops 814022656 | bytes 10488832 | tf_op jit(solution)/shard_map/xyz,yk->xkz/dot_general | solution.py:90
  162.7 4.3 copy.28
  167.0 10.4 %all-to-all-start.1 = ((bf16[32,256,128]{2,0,1:T(8,128)(2,1)}), bf16[32,256,128]{2,0,1:T(8,128)(2,1)}, u32[]{:S(2)}, u32[]{:S(2)}) async-start(bf16[32,256,128]{2,0,1:T(8,128)(2,1)} %copy.28), calls=%async_computation.1 | async-start | bytes 4194304 | tf_op jit(solution)/shard_map/all_to_all | solution.py:93
  177.7 26.0 %all-to-all-done.1 = bf16[32,256,128]{2,0,1:T(8,128)(2,1)} async-done(((bf16[32,256,128]{2,0,1:T(8,128)(2,1)}), bf16[32,256,128]{2,0,1:T(8,128)(2,1)}, u32[]{:S(2)}, u32[]{:S(2)}) %all-to-all-start.1) | async-done | bytes 2097184 | tf_op jit(solution)/shard_map/all_to_all | solution.py:93
  203.7 3.7 copy.30
  207.4 6.9 %fusion.32 = bf16[256,32,128]{2,0,1:T(8,128)(2,1)} fusion(f32[128]{0:T(128)S(1)} %multiply_subtract_fusion.1, f32[256,32]{0,1:T(8,128)S(1)} %broadcast_add_fusion, bf16[256,32,128]{2,1,0:T(8,128)(2,1)} %bitcast.152, f32[256]{0:T(256)S(1)} %get-tuple-element.119, f32[256]{0:T(256)S(1)} %get-tuple-element.120), kind=kOutput, calls=%fused_computation.47 | convolution fusion | flops 1080557568 | bytes 4229632 | tf_op jit(solution)/shard_map/xyz,xk->kyz/dot_general | solution.py:103
  214.2 2.9 copy.32
  217.2 29.6 %all_to_all.82 = bf16[256,32,128]{2,1,0:T(8,128)(2,1)S(1)} all-to-all(bf16[256,32,128]{2,1,0:T(8,128)(2,1)S(1)} %copy.32), channel_id=1, replica_groups=mesh['box'=32,'pencil'=8] {'pencil'}, dimensions={0} | all-to-all | bytes 4194304 | tf_op jit(solution)/shard_map/all_to_all | solution.py:106
  248.7 6.5 %fusion.171 = (f32[32,256,128]{2,1,0:T(8,128)}, bf16[32,256,128]{2,1,0:T(8,128)(2,1)}) fusion(f32[128]{0:T(128)S(1)} %get-tuple-element.121, f32[128]{0:T(128)S(1)} %get-tuple-element.122, bf16[32,256,128]{2,1,0:T(8,128)(2,1)} %bitcast.144, f32[256]{0:T(256)S(1)} %get-tuple-element.119, f32[256]{0:T(256)S(1)} %get-tuple-element.120), kind=kOutput, calls=%fused_computation.160 | convolution fusion | flops 808779776 | bytes 8391680 | tf_op jit(solution)/shard_map/xyz,zk->xyk/dot_general | solution.py:110
  257.3 97.3 %all_to_all.83 = bf16[32,32,16,128]{3,2,1,0:T(8,128)(2,1)} all-to-all(bf16[32,32,16,128]{3,2,1,0:T(8,128)(2,1)S(1)} %stack.5), channel_id=1, replica_groups=mesh['box'=32,'pencil'=8] {'box'}, dimensions={0} | all-to-all | bytes 8388608 | tf_op jit(solution)/shard_map/all_to_all | solution.py:61
  358.5 2.4 scatter-add.34
  362.6 3.7 multiply_add_fusion
  368.3 2.6 fusion.1
  370.9 10.9 %scatter-add.36 = f32[32,256,128]{2,1,0:T(8,128)} dynamic-update-slice(f32[32,256,128]{2,1,0:T(8,128)} %copy-done, f32[32,256,1]{2,1,0:T(8,128)} %fusion.1, s32[]{:T(128)} %constant.259.clone.1, s32[]{:T(128)} %constant.259.clone.1, s32[]{:T(128)} %constant.259.clone.1) | dynamic-update-slice | bytes 65540 | tf_op jit(solution)/shard_map/scatter-add | solution.py:84
  381.8 7.7 %fusion = f32[32,256,1]{2,1,0:T(8,128)} fusion(f32[32,256,128]{2,1,0:T(8,128)} %get-tuple-element.115, f32[32,256,128]{2,1,0:T(8,128)} %scatter-add.36), kind=kLoop, calls=%fused_computation.5 | loop fusion | flops 16384 | bytes 98304 | tf_op jit(solution)/shard_map/add | solution.py:85
  389.5 13.0 %scatter-add.39 = f32[32,256,128]{2,1,0:T(8,128)} dynamic-update-slice(f32[32,256,128]{2,1,0:T(8,128)} %scatter-add.36, f32[32,256,1]{2,1,0:T(8,128)} %fusion, s32[]{:T(128)} %constant.259.clone.1, s32[]{:T(128)} %constant.259.clone.1, s32[]{:T(128)} %constant.270.clone.1) | dynamic-update-slice | bytes 65540 | tf_op jit(solution)/shard_map/scatter-add | solution.py:85
  402.5 6.7 %convert_bitcast_fusion = bf16[32,256,128]{2,1,0:T(8,128)(2,1)} fusion(f32[32,256,128]{2,1,0:T(8,128)} %scatter-add.39, bf16[1,32,256,128]{3,2,1,0:T(8,128)(2,1)} %param.22, f32[256]{0:T(256)S(1)} %get-tuple-element.119, f32[256]{0:T(256)S(1)} %get-tuple-element.120, f32[128]{0:T(128)S(1)} %get-tuple-element.121, f32[128]{0:T(128)S(1)} %get-tuple-element.122, ...), kind=kOutput, calls=%fused_computation.33 | convolution fusion | flops 814022656 | bytes 10488832 | tf_op jit(solution)/shard_map/xyz,yk->xkz/dot_general | solution.py:90
  409.2 2.9 copy.34
  412.1 33.4 %all_to_all.84 = bf16[32,256,128]{2,0,1:T(8,128)(2,1)S(1)} all-to-all(bf16[32,256,128]{2,0,1:T(8,128)(2,1)S(1)} %copy.34), channel_id=1, replica_groups=mesh['box'=32,'pencil'=8] {'pencil'}, dimensions={1} | all-to-all | bytes 4194304 | tf_op jit(solution)/shard_map/all_to_all | solution.py:93
  446.4 5.2 %fusion.31 = bf16[256,32,128]{2,0,1:T(8,128)(2,1)} fusion(f32[128]{0:T(128)S(1)} %multiply_subtract_fusion.1, f32[256,32]{0,1:T(8,128)S(1)} %broadcast_add_fusion, bf16[256,32,128]{2,1,0:T(8,128)(2,1)S(1)} %bitcast.151, f32[256]{0:T(256)S(1)} %get-tuple-element.119, f32[256]{0:T(256)S(1)} %get-tuple-element.120), kind=kOutput, calls=%fused_computation.46 | convolution fusion | flops 1080557568 | bytes 4229632 | tf_op jit(solution)/shard_map/xyz,xk->kyz/dot_general | solution.py:103
  451.6 2.9 copy.38
  454.5 29.6 %all_to_all.85 = bf16[256,32,128]{2,1,0:T(8,128)(2,1)S(1)} all-to-all(bf16[256,32,128]{2,1,0:T(8,128)(2,1)S(1)} %copy.38), channel_id=1, replica_groups=mesh['box'=32,'pencil'=8] {'pencil'}, dimensions={0} | all-to-all | bytes 4194304 | tf_op jit(solution)/shard_map/all_to_all | solution.py:106
  484.8 4.2 convolution_bitcast_fusion
  (52 shorter events, 24.6 us)
Async XLA Ops:
  4.0 12.2 %copy-start.5 = (s32[32,2,16]{0,2,1:T(8,128)S(1)}, s32[32,2,16]{0,2,1:T(8,128)}, u32[]{:S(2)}) copy-start(s32[32,2,16]{0,2,1:T(8,128)} %param.24) | copy-start | bytes 12292
  4.0 12.2 %copy-start.6 = (s32[32,2,16]{0,2,1:T(8,128)S(1)}, s32[32,2,16]{0,2,1:T(8,128)}, u32[]{:S(2)}) copy-start(s32[32,2,16]{0,2,1:T(8,128)} %param.23) | copy-start | bytes 12292
  4.1 12.5 %copy-start.7 = (s32[1,2,32]{2,1,0:T(2,128)S(1)}, s32[1,2,32]{2,1,0:T(2,128)}, u32[]{:S(2)}) copy-start(s32[1,2,32]{2,1,0:T(2,128)} %param.25) | copy-start | bytes 772
  4.1 12.6 %copy-start.4 = (bf16[1,32,256,128]{3,2,1,0:T(8,128)(2,1)S(1)}, bf16[1,32,256,128]{3,2,1,0:T(8,128)(2,1)}, u32[]{:S(2)}) copy-start(bf16[1,32,256,128]{3,2,1,0:T(8,128)(2,1)} %param.21) | copy-start | bytes 6291460
  4.1 104.7 %all-to-all-start = ((bf16[32,32,16,128]{3,2,1,0:T(8,128)(2,1)}), bf16[32,32,16,128]{3,2,1,0:T(8,128)(2,1)}, u32[]{:S(2)}, u32[]{:S(2)}) async-start(bf16[32,32,16,128]{3,2,1,0:T(8,128)(2,1)} %stack.4), calls=%async_computation | async-start | bytes 8388608 | tf_op jit(solution)/shard_map/all_to_all | solution.py:61
  116.7 5.1 %copy-start.3 = (f32[32,256,128]{2,1,0:T(8,128)S(1)}, f32[32,256,128]{2,1,0:T(8,128)}, u32[]{:S(2)}) copy-start(f32[32,256,128]{2,1,0:T(8,128)} %bitcast_convert_fusion) | copy-start | bytes 12582916
  119.8 2.0 copy-start.1
  167.0 36.7 %all-to-all-start.1 = ((bf16[32,256,128]{2,0,1:T(8,128)(2,1)}), bf16[32,256,128]{2,0,1:T(8,128)(2,1)}, u32[]{:S(2)}, u32[]{:S(2)}) async-start(bf16[32,256,128]{2,0,1:T(8,128)(2,1)} %copy.28), calls=%async_computation.1 | async-start | bytes 4194304 | tf_op jit(solution)/shard_map/all_to_all | solution.py:93
  362.6 5.7 %copy-start.2 = (f32[32,256,128]{2,1,0:T(8,128)S(1)}, f32[32,256,128]{2,1,0:T(8,128)}, u32[]{:S(2)}) copy-start(f32[32,256,128]{2,1,0:T(8,128)} %get-tuple-element.115) | copy-start | bytes 12582916
  366.3 2.0 copy-start
